TPU v7x, 512 devices: a whole 4x8x8 slice. The times are simulated.
512 devices in a mesh: blk: 64 (over x, z_hi, y), grp: 8 (over z_lo, core).
Axes of the slice: x: 4, y: 8, z: 8 (z_hi: 2, z_lo: 4; z = z_hi * 4 + z_lo), core: 2. Of those that a mesh axis runs over, the one named last changes fastest.
Arguments:
- excitation: bfloat16 [128, 1024, 256], P('blk'), may hold values from -6 to 6
- inverse_self: bfloat16 [128, 1024, 1024], P('blk', 'grp'), may hold values from -0.1875 to 0.1875
- coupling: bfloat16 [128, 4, 1024, 1024], P('blk', None, 'grp'), may hold values from -0.1875 to 0.1875
- neighbour_mask: int32 [128, 4], P('blk'), may hold values 0 or 1
- sketch: float32 [5, 256, 32], replicated, may hold values from -6 to 6
Outputs:
- bases: float32 [128, 1024, 32], P('blk', 'grp')
- reduced_coupling: float32 [128, 4, 32, 32], P('blk')
- reduced_excitation: float32 [128, 32, 256], P('blk')
Inputs may be any that keep to these rules, and one draw needn't show every extreme that they name: `neighbour_mask`: 1 where the block at that slot's offset adds secondary currents, 0 where it does not; slots pointing outside the array add nothing in any case.
All inputs are finite; a program needn't handle non-finite values.
Results may differ from a plain program's by a relative error of at most 0.0003.
Values sent between devices are 32-bit elements; how exact they have to be, the bound alone decides.
No kernel may reach another device: no remote copies, remote signals or barrier semaphores. Data moves between devices by JAX's collectives and lax.ppermute only.
A program may use at most 64 MiB of HBM per device.

v0:
```python
import math
import jax
import jax.numpy as jnp
from jax import lax
from jax.sharding import PartitionSpec as P

neighbour_offsets = (-2, -1, 1, 2)


def extended(array, sides, width):
    for axis, dim in sides:
        size, length = (lax.axis_size(axis), array.shape[dim])
        up = [(i, (i + 1) % size) for i in range(size - 1)]
        down = [(j, i) for i, j in up]
        last = lax.slice_in_dim(array, length - width, length, axis=dim)
        initial = lax.slice_in_dim(array, 0, width, axis=dim)
        before = lax.ppermute(last, axis, up)
        after = lax.ppermute(initial, axis, down)
        array = jnp.concatenate([before, array, after], axis=dim)
    return array


def exact_einsum(form, left, right):
    return jnp.einsum(
        form, left, right, precision=lax.Precision.HIGHEST, preferred_element_type=jnp.float32
    )


def shards(excitation, inverse_self, coupling, neighbour_mask, sketch):
    blocks, unknowns, columns = excitation.shape
    shard_rows = inverse_self.shape[1]
    retained = sketch.shape[2]
    row_start = lax.axis_index("grp") * shard_rows
    own_excitation = lax.dynamic_slice_in_dim(excitation, row_start, shard_rows, 1)
    primary = jnp.einsum(
        "bnm,bmp->bnp", inverse_self, excitation, preferred_element_type=jnp.float32
    )
    weights_mask = neighbour_mask.astype(jnp.float32)
    own_whole = lax.all_gather(primary, "grp", axis=1, tiled=True)
    nearby = extended(own_whole, (("blk", 0),), 2)
    sources = jnp.zeros((blocks, shard_rows, retained), jnp.float32)
    for slot_index, offset in enumerate(neighbour_offsets):
        neighbour = nearby[2 + offset : 2 + offset + blocks]
        coupled_full = exact_einsum("bnm,bmp->bnp", coupling[:, slot_index], neighbour)
        coupled_term = exact_einsum("bnp,pr->bnr", coupled_full, sketch[slot_index + 1])
        sources = sources + weights_mask[:, slot_index, None, None] * coupled_term
    all_sources = lax.all_gather(sources, "grp", axis=1, tiled=True)
    sketched = exact_einsum("bnp,pr->bnr", primary, sketch[0]) - exact_einsum(
        "bnm,bmr->bnr", inverse_self, all_sources
    )
    gram_part = exact_einsum("bnr,bns->brs", sketched, sketched)
    gram_total = lax.psum(gram_part, "grp") / unknowns
    chol_lower = jnp.linalg.cholesky(gram_total)
    bases = lax.linalg.triangular_solve(
        chol_lower, sketched, left_side=False, lower=True, transpose_a=True
    )
    basis_shards = extended(bases, (("blk", 0),), 2)
    basis_near = lax.all_gather(basis_shards, "grp", axis=1, tiled=True)
    stacked = []
    for slot_index, offset in enumerate(neighbour_offsets):
        coupled_basis = exact_einsum(
            "bnm,bmr->bnr", coupling[:, slot_index], basis_near[2 + offset : 2 + offset + blocks]
        )
        stacked.append(exact_einsum("bnr,bns->brs", bases, coupled_basis))
    coupled_part = jnp.stack(stacked, axis=1)
    driven_part = exact_einsum("bnr,bnp->brp", bases, own_excitation)
    coupled_sum, driven_sum = lax.psum((coupled_part, driven_part), "grp")
    norm_scale = 1.0 / math.sqrt(unknowns)
    return (bases, coupled_sum * norm_scale, driven_sum * norm_scale)


def solution(mesh):
    return jax.shard_map(
        shards,
        mesh=mesh,
        in_specs=(
            P("blk", None, None),
            P("blk", "grp", None),
            P("blk", None, "grp", None),
            P("blk", None),
            P(),
        ),
        out_specs=(P("blk", "grp", None), P("blk", None, None, None), P("blk", None, None)),
        check_vma=False,
    )
```

profile of v0, /device:TPU:2, one launch (start us, length us, event | category | flops | bytes accessed | tf_op | source)
XLA Modules:
  0.0 315.8 jit_solution(14222659182359712413)
XLA Ops:
  7.2 0.0 copy-start
  7.2 0.0 all-gather.2.cloned.1.call-start
  7.3 1.1 copy-done
  8.4 2.1 fusion.57
  10.5 0.0 all-gather.2.cloned.1.call-update
  10.5 0.0 all-reduce.2.cloned.1.call-start
  10.5 46.6 %all-gather.2.cloned.1.call-done = f32[2,1024,256]{2,1,0:T(8,128)} async-done(((f32[2,128,256]{2,1,0:T(8,128)}), f32[2,1024,256]{2,1,0:T(8,128)}) %all-gather.2.cloned.1.call-update) | async-done | bytes 2097168 | tf_op jit(solution)/shard_map/all_gather | solution.py:39
  57.1 3.4 %collective-permute-start = (f32[2,1024,256]{2,1,0:T(8,128)}, f32[2,1024,256]{2,1,0:T(8,128)}, u32[]{:S(2)}, u32[]{:S(2)}) collective-permute-start(f32[2,1024,256]{2,1,0:T(8,128)} %all-gather.2.cloned.1.call-done), channel_id=1, source_target_pairs={{0,8},{8,16},{16,24},{24,32},{32,40},{40,48},{48,56},{56,64},{64,7... | collective-permute-start | bytes 6291464 | tf_op jit(solution)/shard_map/ppermute | solution.py:17
  60.5 9.4 %collective-permute-start.1 = (f32[2,1024,256]{2,1,0:T(8,128)}, f32[2,1024,256]{2,1,0:T(8,128)}, u32[]{:S(2)}, u32[]{:S(2)}) collective-permute-start(f32[2,1024,256]{2,1,0:T(8,128)} %all-gather.2.cloned.1.call-done), channel_id=1, source_target_pairs={{8,0},{16,8},{24,16},{32,24},{40,32},{48,40},{56,48},{64,56},{72,6... | collective-permute-start | bytes 6291464 | tf_op jit(solution)/shard_map/ppermute | solution.py:18
  70.0 0.2 slice_reduce_fusion
  70.2 1.4 fusion.47
  71.6 85.4 %collective-permute-done = f32[2,1024,256]{2,1,0:T(8,128)} collective-permute-done((f32[2,1024,256]{2,1,0:T(8,128)}, f32[2,1024,256]{2,1,0:T(8,128)}, u32[]{:S(2)}, u32[]{:S(2)}) %collective-permute-start) | collective-permute-done | bytes 2097184 | tf_op jit(solution)/shard_map/ppermute | solution.py:17
  157.0 3.4 %convolution_bitcast_fusion.1 = f32[2,128,256]{1,2,0:T(8,128)S(1)} fusion(f32[2,1024,256]{2,1,0:T(8,128)} %collective-permute-done, bf16[2,4,128,1024]{3,2,1,0:T(8,128)(2,1)S(1)} %copy-done.1), kind=kOutput, calls=%fused_computation.11 | convolution fusion | flops 805306368 | bytes 2883584 | tf_op jit(solution)/shard_map/bnm,bmp->bnp/dot_general | solution.py:24
  160.5 0.3 convolution_multiply_fusion.3
  160.8 3.0 fusion.11
  163.8 0.3 fusion.17
  164.1 3.0 fusion.8
  167.1 0.3 fusion.16
  167.4 3.4 %convolution_bitcast_fusion = f32[2,128,256]{1,2,0:T(8,128)S(1)} fusion(f32[2,1024,256]{2,1,0:T(8,128)} %collective-permute-done.1, bf16[2,4,128,1024]{3,2,1,0:T(8,128)(2,1)S(1)} %copy-done.1), kind=kOutput, calls=%fused_computation.10 | convolution fusion | flops 805306368 | bytes 2883584 | tf_op jit(solution)/shard_map/bnm,bmp->bnp/dot_general | solution.py:24
  170.8 0.3 fusion.15
  171.1 14.2 %all_gather.10 = f32[2,1024,32]{1,2,0:T(8,128)S(1)} all-gather(f32[2,128,32]{1,2,0:T(8,128)S(1)} %fusion.15), channel_id=1, replica_groups=mesh['blk'=64,'grp'=8] {'grp'}, dimensions={1}, use_global_device_ids=true | all-gather | bytes 294912 | tf_op jit(solution)/shard_map/all_gather | solution.py:47
  185.3 0.6 fusion.14
  185.9 0.2 fusion.58
  186.1 26.2 %psum.21 = f32[2,32,32]{1,2,0:T(8,128)S(1)} all-reduce(f32[2,32,32]{1,2,0:T(8,128)S(1)} %fusion.58), channel_id=1, replica_groups=mesh['blk'=64,'grp'=8] {'grp'}, use_global_device_ids=true, to_apply=%region_0.0 | all-reduce | flops 2048 | bytes 16384 | tf_op jit(solution)/shard_map/psum | solution.py:52
  212.3 0.1 copy.13
  212.4 5.9 %custom-call.7 = f32[2,32,32]{2,1,0:T(8,128)S(1)} custom-call(f32[2,32,32]{2,1,0:T(8,128)S(1)} %fusion.42), custom_call_target="Cholesky" | custom-call | tf_op jit(solution)/shard_map/jit(cholesky)/cholesky | solution.py:53
  218.3 0.1 compare_reduce_fusion
  218.4 0.1 select_bitcast_fusion
  218.5 4.9 %custom-call.8 = f32[2,1,32,32]{2,3,1,0:T(8,128)S(1)} custom-call(f32[2,1,32,32]{3,2,1,0:T(8,128)S(1)} %select_bitcast_fusion), custom_call_target="InvertDiagBlocksLowerTriangular" | custom-call | tf_op jit(solution)/shard_map/triangular_solve | solution.py:54
  223.4 0.3 fusion.40
  223.7 5.4 %collective-permute-start.3 = (f32[2,128,32]{1,2,0:T(8,128)S(1)}, f32[2,128,32]{1,2,0:T(8,128)S(1)}, u32[]{:S(2)}, u32[]{:S(2)}) collective-permute-start(f32[2,128,32]{1,2,0:T(8,128)S(1)} %fusion.40), channel_id=1, source_target_pairs={{8,0},{16,8},{24,16},{32,24},{40,32},{48,40},{56,48},{64,56},{72,6... | collective-permute-start | bytes 98312 | tf_op jit(solution)/shard_map/ppermute | solution.py:18
  229.1 1.9 collective-permute-start.2
  231.0 0.8 fusion.38
  231.9 0.0 all-reduce.2.cloned.1.call-update
  231.9 10.0 %collective-permute-done.2 = f32[2,128,32]{1,2,0:T(8,128)S(1)} collective-permute-done((f32[2,128,32]{1,2,0:T(8,128)S(1)}, f32[2,128,32]{1,2,0:T(8,128)S(1)}, u32[]{:S(2)}, u32[]{:S(2)}) %collective-permute-start.2) | collective-permute-done | bytes 32800 | tf_op jit(solution)/shard_map/ppermute | solution.py:17
  241.9 16.0 %all_gather.11 = f32[6,1024,32]{1,2,0:T(8,128)S(1)} all-gather(f32[6,128,32]{1,2,0:T(8,128)S(1)} %pad_maximum_fusion.1), channel_id=1, replica_groups=mesh['blk'=64,'grp'=8] {'grp'}, dimensions={1}, use_global_device_ids=true | all-gather | bytes 884736 | tf_op jit(solution)/shard_map/all_gather | solution.py:58
  257.9 0.6 fusion.18
  258.5 0.6 fusion.21
  259.1 0.6 fusion.24
  259.8 0.6 fusion.27
  260.4 0.2 convolution_bitcast_fusion.2
  260.6 0.2 convolution_bitcast_fusion.3
  260.7 0.2 convolution_bitcast_fusion.4
  260.9 0.2 convolution_bitcast_fusion.5
  261.1 27.9 %psum.22 = f32[2,4,32,32]{3,2,0,1:T(8,128)S(1)} all-reduce(f32[2,4,32,32]{3,2,0,1:T(8,128)S(1)} %pad_maximum_fusion), channel_id=1, replica_groups=mesh['blk'=64,'grp'=8] {'grp'}, use_global_device_ids=true, to_apply=%region_3.4 | all-reduce | flops 8192 | bytes 65536 | tf_op jit(solution)/shard_map/psum | solution.py:67
  289.1 0.7 copy.15
  289.7 17.8 %all-reduce.2.cloned.1.call-done = f32[2,32,256]{2,1,0:T(8,128)} async-done(((f32[2,32,256]{2,1,0:T(8,128)}), f32[2,32,256]{2,1,0:T(8,128)}) %all-reduce.2.cloned.1.call-update) | async-done | bytes 65552 | tf_op jit(solution)/shard_map/psum | solution.py:67
  307.5 1.5 broadcast_multiply_fusion.1
  (23 shorter events, 0.1 us)
Async XLA Ops:
  7.2 1.2 copy-start
  7.2 62.7 %copy-start.6 = (s32[2,4]{1,0:T(2,128)S(1)}, s32[2,4]{1,0:T(2,128)}, u32[]{:S(2)}) copy-start(s32[2,4]{1,0:T(2,128)} %param.8) | copy-start | bytes 100
  7.2 63.0 %copy-start.5 = (f32[5,256,32]{1,2,0:T(8,128)S(1)}, f32[5,256,32]{1,2,0:T(8,128)}, u32[]{:S(2)}) copy-start(f32[5,256,32]{1,2,0:T(8,128)} %param.9) | copy-start | bytes 491524
  7.2 149.8 %copy-start.1 = (bf16[2,4,128,1024]{3,2,1,0:T(8,128)(2,1)S(1)}, bf16[2,4,128,1024]{3,2,1,0:T(8,128)(2,1)}, u32[]{:S(2)}) copy-start(bf16[2,4,128,1024]{3,2,1,0:T(8,128)(2,1)} %param.7) | copy-start | bytes 6291460
  7.2 49.9 %all-gather.2.cloned.1.call-start = ((), (), s32[]{:S(2)}) async-start(), calls=%async_computation | async-start | bytes 2359296 | tf_op jit(solution)/shard_map/all_gather | solution.py:39
  10.5 297.0 %all-reduce.2.cloned.1.call-start = ((), (), s32[]{:S(2)}) async-start(), calls=%async_computation.1 | async-start | bytes 131072 | tf_op jit(solution)/shard_map/psum | solution.py:67
  57.1 99.9 %collective-permute-start = (f32[2,1024,256]{2,1,0:T(8,128)}, f32[2,1024,256]{2,1,0:T(8,128)}, u32[]{:S(2)}, u32[]{:S(2)}) collective-permute-start(f32[2,1024,256]{2,1,0:T(8,128)} %all-gather.2.cloned.1.call-done), channel_id=1, source_target_pairs={{0,8},{8,16},{16,24},{24,32},{32,40},{40,48},{48,56},{56,64},{64,7... | collective-permute-start | bytes 6291464 | tf_op jit(solution)/shard_map/ppermute | solution.py:17
  60.5 103.6 %collective-permute-start.1 = (f32[2,1024,256]{2,1,0:T(8,128)}, f32[2,1024,256]{2,1,0:T(8,128)}, u32[]{:S(2)}, u32[]{:S(2)}) collective-permute-start(f32[2,1024,256]{2,1,0:T(8,128)} %all-gather.2.cloned.1.call-done), channel_id=1, source_target_pairs={{8,0},{16,8},{24,16},{32,24},{40,32},{48,40},{56,48},{64,56},{72,6... | collective-permute-start | bytes 6291464 | tf_op jit(solution)/shard_map/ppermute | solution.py:18
  69.9 90.8 %copy-start.2 = (f32[2,1024,256]{2,1,0:T(8,128)S(1)}, f32[2,1024,256]{2,1,0:T(8,128)}, u32[]{:S(2)}) copy-start(f32[2,1024,256]{2,1,0:T(8,128)} %all-gather.2.cloned.1.call-done) | copy-start | bytes 6291460
  167.1 18.2 %copy-start.3 = (bf16[2,128,1024]{2,1,0:T(8,128)(2,1)S(1)}, bf16[2,128,1024]{2,1,0:T(8,128)(2,1)}, u32[]{:S(2)}) copy-start(bf16[2,128,1024]{2,1,0:T(8,128)(2,1)} %param.6) | copy-start | bytes 1572868
  223.7 37.2 %copy-start.4 = (f32[2,128,32]{1,2,0:T(8,128)}, f32[2,128,32]{1,2,0:T(8,128)S(1)}, u32[]{:S(2)}) copy-start(f32[2,128,32]{1,2,0:T(8,128)S(1)} %fusion.40) | copy-start | bytes 98308
  223.7 8.2 %collective-permute-start.3 = (f32[2,128,32]{1,2,0:T(8,128)S(1)}, f32[2,128,32]{1,2,0:T(8,128)S(1)}, u32[]{:S(2)}, u32[]{:S(2)}) collective-permute-start(f32[2,128,32]{1,2,0:T(8,128)S(1)} %fusion.40), channel_id=1, source_target_pairs={{8,0},{16,8},{24,16},{32,24},{40,32},{48,40},{56,48},{64,56},{72,6... | collective-permute-start | bytes 98312 | tf_op jit(solution)/shard_map/ppermute | solution.py:18
  229.1 12.8 %collective-permute-start.2 = (f32[2,128,32]{1,2,0:T(8,128)S(1)}, f32[2,128,32]{1,2,0:T(8,128)S(1)}, u32[]{:S(2)}, u32[]{:S(2)}) collective-permute-start(f32[2,128,32]{1,2,0:T(8,128)S(1)} %fusion.40), channel_id=1, source_target_pairs={{0,8},{8,16},{16,24},{24,32},{32,40},{40,48},{48,56},{56,64},{64,7... | collective-permute-start | bytes 98312 | tf_op jit(solution)/shard_map/ppermute | solution.py:17
Sparse Core Ops, SparseCore 0:
  10.6 46.4 all-gather.1
  232.0 75.4 all-reduce.1
where the time goes:
time: 316 us
  waiting for transfers between devices  160 us (51%)
  blocking collectives  84.3 us (27%)
  matrix products  22.4 us (7%)
  starting transfers between devices  20.1 us (6%)
  between operations  14.4 us (5%)
  other arithmetic  12.5 us (4%)
    ppermute x2, waiting for transfers between devices, extended(): before = lax.ppermute(last, axis, up)  95.5 us
    all_gather x1, waiting for transfers between devices, shards(): own_whole = lax.all_gather(primary, 'grp', axis=1, tiled=True)  46.6 us
    psum x1, blocking collectives, shards(): coupled_sum, driven_sum = lax.psum((coupled_part, driven_part), 'grp')  27.9 us
    psum x1, blocking collectives, shards(): gram_total = lax.psum(gram_part, 'grp') / unknowns  26.2 us
    dot_general x20, matrix products, exact_einsum(): jnp.einsum(form, left, right, precision=lax.Precision.HIGHEST, preferred_...  20.1 us
    psum x1, waiting for transfers between devices, shards(): coupled_sum, driven_sum = lax.psum((coupled_part, driven_part), 'grp')  17.8 us
    all_gather x1, blocking collectives, shards(): basis_near = lax.all_gather(basis_shards, 'grp', axis=1, tiled=True)  16 us
    ppermute x2, starting transfers between devices, extended(): after = lax.ppermute(initial, axis, down)  14.8 us
  transfers between devices with their start and end apart: 6, of which 4 were waited for; matrix products, arithmetic and copies ran while one was open for 4% of the time, Pallas kernels for 0%

commit v1 on v0

--- a/solution.py
+++ b/solution.py
@@ -36,7 +36,9 @@
         "bnm,bmp->bnp", inverse_self, excitation, preferred_element_type=jnp.float32
     )
     weights_mask = neighbour_mask.astype(jnp.float32)
-    own_whole = lax.all_gather(primary, "grp", axis=1, tiled=True)
+    own_whole = jnp.concatenate(
+        lax.all_to_all(jnp.stack([primary] * lax.axis_size("grp")), "grp", 0, 0), axis=1
+    )
     nearby = extended(own_whole, (("blk", 0),), 2)
     sources = jnp.zeros((blocks, shard_rows, retained), jnp.float32)
     for slot_index, offset in enumerate(neighbour_offsets):

time: 316 us -> 331 us (1.047)
  blocking collectives: 84.3 us -> 143 us
  waiting for transfers between devices: 160 us -> 116 us
  matrix products: 22.4 us -> 18.6 us
  local copies, waits for them, and re-layouts: 2.13 us -> 5.8 us
    all_to_all x0 -> x1, blocking collectives: none -> 56.1 us  [shards(): lax.all_to_all(jnp.stack([primary] * lax.axis_size('grp')), 'grp', 0, 0)]
    all_gather x1 -> x0, waiting for transfers between devices: 46.6 us -> none  [shards(): own_whole = lax.all_gather(primary, 'grp', axis=1, tiled=True)]
  transfers between devices with their start and end apart: 6 -> 5, of which waited for: 4 -> 3; matrix products, arithmetic and copies ran while one was open for 4% -> 4% of each run, Pallas kernels for 0% -> 0%
where the time goes in v1:
time: 331 us
  blocking collectives  143 us (43%)
  waiting for transfers between devices  116 us (35%)
  starting transfers between devices  20.5 us (6%)
  matrix products  18.6 us (6%)
  between operations  14.4 us (4%)
  other arithmetic  12.5 us (4%)
  local copies, waits for them, and re-layouts  5.8 us (2%)
    ppermute x2, waiting for transfers between devices, extended(): before = lax.ppermute(last, axis, up)  97.2 us
    all_to_all x1, blocking collectives, shards(): lax.all_to_all(jnp.stack([primary] * lax.axis_size('grp')), 'grp', 0, 0)  56.1 us
    psum x1, blocking collectives, shards(): gram_total = lax.psum(gram_part, 'grp') / unknowns  29.1 us
    psum x1, blocking collectives, shards(): coupled_sum, driven_sum = lax.psum((coupled_part, driven_part), 'grp')  28 us
    psum x1, waiting for transfers between devices, shards(): coupled_sum, driven_sum = lax.psum((coupled_part, driven_part), 'grp')  18.3 us
    dot_general x20, matrix products, exact_einsum(): jnp.einsum(form, left, right, precision=lax.Precision.HIGHEST, preferred_...  17 us
    all_gather x1, blocking collectives, shards(): basis_near = lax.all_gather(basis_shards, 'grp', axis=1, tiled=True)  15.7 us
    ppermute x2, starting transfers between devices, extended(): after = lax.ppermute(initial, axis, down)  15 us
  transfers between devices with their start and end apart: 5, of which 3 were waited for; matrix products, arithmetic and copies ran while one was open for 4% of the time, Pallas kernels for 0%

profile of v1, /device:TPU:2, one launch (start us, length us, event | category | flops | bytes accessed | tf_op | source)
XLA Modules:
  0.0 330.7 jit_solution(14445957119212141808)
XLA Ops:
  7.2 0.0 all-reduce.2.cloned.1.call-start
  7.2 1.2 copy-done
  8.4 1.3 fusion.57
  9.7 0.2 stack.12
  9.9 56.1 %all_to_all.5 = f32[8,2,128,256]{3,2,1,0:T(8,128)S(1)} all-to-all(f32[8,2,128,256]{3,2,1,0:T(8,128)S(1)} %stack.12), channel_id=1, replica_groups=mesh['blk'=64,'grp'=8] {'grp'}, dimensions={0} | all-to-all | bytes 4194304 | tf_op jit(solution)/shard_map/all_to_all | solution.py:40
  66.0 1.5 copy.33
  67.5 1.9 copy.34
  69.5 3.5 %collective-permute-start = (f32[2,1024,256]{1,2,0:T(8,128)S(1)}, f32[2,1024,256]{1,2,0:T(8,128)}, u32[]{:S(2)}, u32[]{:S(2)}) collective-permute-start(f32[2,1024,256]{1,2,0:T(8,128)S(1)} %copy.34), channel_id=1, source_target_pairs={{0,8},{8,16},{16,24},{24,32},{32,40},{40,48},{48,56},{56,64},{64,7... | collective-permute-start | bytes 6291464 | tf_op jit(solution)/shard_map/ppermute | solution.py:17
  73.0 9.5 %collective-permute-start.1 = (f32[2,1024,256]{1,2,0:T(8,128)S(1)}, f32[2,1024,256]{1,2,0:T(8,128)}, u32[]{:S(2)}, u32[]{:S(2)}) collective-permute-start(f32[2,1024,256]{1,2,0:T(8,128)S(1)} %copy.34), channel_id=1, source_target_pairs={{8,0},{16,8},{24,16},{32,24},{40,32},{48,40},{56,48},{64,56},{72,6... | collective-permute-start | bytes 6291464 | tf_op jit(solution)/shard_map/ppermute | solution.py:18
  82.6 0.2 slice_reduce_fusion
  82.8 1.3 fusion.47
  84.1 87.3 %collective-permute-done = f32[2,1024,256]{1,2,0:T(8,128)} collective-permute-done((f32[2,1024,256]{1,2,0:T(8,128)S(1)}, f32[2,1024,256]{1,2,0:T(8,128)}, u32[]{:S(2)}, u32[]{:S(2)}) %collective-permute-start) | collective-permute-done | bytes 2097184 | tf_op jit(solution)/shard_map/ppermute | solution.py:17
  171.4 2.7 convolution_bitcast_fusion.1
  174.1 0.3 convolution_multiply_fusion.3
  174.4 2.3 fusion.11
  176.7 0.3 fusion.17
  177.0 2.3 fusion.8
  179.3 0.3 fusion.16
  179.5 2.7 convolution_bitcast_fusion
  182.2 0.3 fusion.15
  182.5 14.4 %all_gather.6 = f32[2,1024,32]{1,2,0:T(8,128)S(1)} all-gather(f32[2,128,32]{1,2,0:T(8,128)S(1)} %fusion.15), channel_id=1, replica_groups=mesh['blk'=64,'grp'=8] {'grp'}, dimensions={1}, use_global_device_ids=true | all-gather | bytes 294912 | tf_op jit(solution)/shard_map/all_gather | solution.py:49
  196.9 0.6 fusion.14
  197.5 0.2 fusion.58
  197.7 29.1 %psum.21 = f32[2,32,32]{1,2,0:T(8,128)S(1)} all-reduce(f32[2,32,32]{1,2,0:T(8,128)S(1)} %fusion.58), channel_id=1, replica_groups=mesh['blk'=64,'grp'=8] {'grp'}, use_global_device_ids=true, to_apply=%region_0.0 | all-reduce | flops 2048 | bytes 16384 | tf_op jit(solution)/shard_map/psum | solution.py:54
  226.8 0.1 copy.47
  226.9 5.9 %custom-call.7 = f32[2,32,32]{2,1,0:T(8,128)S(1)} custom-call(f32[2,32,32]{2,1,0:T(8,128)S(1)} %fusion.42), custom_call_target="Cholesky" | custom-call | tf_op jit(solution)/shard_map/jit(cholesky)/cholesky | solution.py:55
  232.8 0.1 compare_reduce_fusion
  232.9 0.1 select_bitcast_fusion
  233.0 4.9 %custom-call.8 = f32[2,1,32,32]{2,3,1,0:T(8,128)S(1)} custom-call(f32[2,1,32,32]{3,2,1,0:T(8,128)S(1)} %select_bitcast_fusion), custom_call_target="InvertDiagBlocksLowerTriangular" | custom-call | tf_op jit(solution)/shard_map/triangular_solve | solution.py:56
  237.9 0.3 fusion.40
  238.2 5.5 %collective-permute-start.3 = (f32[2,128,32]{1,2,0:T(8,128)S(1)}, f32[2,128,32]{1,2,0:T(8,128)S(1)}, u32[]{:S(2)}, u32[]{:S(2)}) collective-permute-start(f32[2,128,32]{1,2,0:T(8,128)S(1)} %fusion.40), channel_id=1, source_target_pairs={{8,0},{16,8},{24,16},{32,24},{40,32},{48,40},{56,48},{64,56},{72,6... | collective-permute-start | bytes 98312 | tf_op jit(solution)/shard_map/ppermute | solution.py:18
  243.7 1.9 collective-permute-start.2
  245.6 0.8 fusion.38
  246.4 0.0 all-reduce.2.cloned.1.call-update
  246.5 10.0 %collective-permute-done.2 = f32[2,128,32]{1,2,0:T(8,128)S(1)} collective-permute-done((f32[2,128,32]{1,2,0:T(8,128)S(1)}, f32[2,128,32]{1,2,0:T(8,128)S(1)}, u32[]{:S(2)}, u32[]{:S(2)}) %collective-permute-start.2) | collective-permute-done | bytes 32800 | tf_op jit(solution)/shard_map/ppermute | solution.py:17
  256.4 15.7 %all_gather.7 = f32[6,1024,32]{1,2,0:T(8,128)S(1)} all-gather(f32[6,128,32]{1,2,0:T(8,128)S(1)} %pad_maximum_fusion.1), channel_id=1, replica_groups=mesh['blk'=64,'grp'=8] {'grp'}, dimensions={1}, use_global_device_ids=true | all-gather | bytes 884736 | tf_op jit(solution)/shard_map/all_gather | solution.py:60
  272.2 0.6 fusion.18
  272.8 0.6 fusion.21
  273.4 0.6 fusion.24
  274.0 0.6 fusion.27
  274.6 0.2 convolution_bitcast_fusion.2
  274.8 0.2 convolution_bitcast_fusion.3
  275.0 0.2 convolution_bitcast_fusion.4
  275.2 0.2 convolution_bitcast_fusion.5
  275.4 28.0 %psum.22 = f32[2,4,32,32]{3,2,0,1:T(8,128)S(1)} all-reduce(f32[2,4,32,32]{3,2,0,1:T(8,128)S(1)} %pad_maximum_fusion), channel_id=1, replica_groups=mesh['blk'=64,'grp'=8] {'grp'}, use_global_device_ids=true, to_apply=%region_3.4 | all-reduce | flops 8192 | bytes 65536 | tf_op jit(solution)/shard_map/psum | solution.py:69
  303.4 0.7 copy.49
  304.1 18.3 %all-reduce.2.cloned.1.call-done = f32[2,32,256]{2,1,0:T(8,128)} async-done(((f32[2,32,256]{2,1,0:T(8,128)}), f32[2,32,256]{2,1,0:T(8,128)}) %all-reduce.2.cloned.1.call-update) | async-done | bytes 65552 | tf_op jit(solution)/shard_map/psum | solution.py:69
  322.4 1.5 broadcast_multiply_fusion.1
  (24 shorter events, 0.1 us)
Async XLA Ops:
  7.2 1.2 copy-start
  7.2 315.2 %all-reduce.2.cloned.1.call-start = ((), (), s32[]{:S(2)}) async-start(), calls=%async_computation.1 | async-start | bytes 131072 | tf_op jit(solution)/shard_map/psum | solution.py:69
  67.5 15.0 %copy-start.6 = (s32[2,4]{1,0:T(2,128)S(1)}, s32[2,4]{1,0:T(2,128)}, u32[]{:S(2)}) copy-start(s32[2,4]{1,0:T(2,128)} %param.8) | copy-start | bytes 100
  69.5 101.9 %collective-permute-start = (f32[2,1024,256]{1,2,0:T(8,128)S(1)}, f32[2,1024,256]{1,2,0:T(8,128)}, u32[]{:S(2)}, u32[]{:S(2)}) collective-permute-start(f32[2,1024,256]{1,2,0:T(8,128)S(1)} %copy.34), channel_id=1, source_target_pairs={{0,8},{8,16},{16,24},{24,32},{32,40},{40,48},{48,56},{56,64},{64,7... | collective-permute-start | bytes 6291464 | tf_op jit(solution)/shard_map/ppermute | solution.py:17
  73.0 104.0 %collective-permute-start.1 = (f32[2,1024,256]{1,2,0:T(8,128)S(1)}, f32[2,1024,256]{1,2,0:T(8,128)}, u32[]{:S(2)}, u32[]{:S(2)}) collective-permute-start(f32[2,1024,256]{1,2,0:T(8,128)S(1)} %copy.34), channel_id=1, source_target_pairs={{8,0},{16,8},{24,16},{32,24},{40,32},{48,40},{56,48},{64,56},{72,6... | collective-permute-start | bytes 6291464 | tf_op jit(solution)/shard_map/ppermute | solution.py:18
  82.6 91.5 %copy-start.5 = (f32[5,256,32]{1,2,0:T(8,128)S(1)}, f32[5,256,32]{1,2,0:T(8,128)}, u32[]{:S(2)}) copy-start(f32[5,256,32]{1,2,0:T(8,128)} %param.9) | copy-start | bytes 491524
  82.6 91.8 %copy-start.1 = (bf16[2,4,128,1024]{3,2,1,0:T(8,128)(2,1)S(1)}, bf16[2,4,128,1024]{3,2,1,0:T(8,128)(2,1)}, u32[]{:S(2)}) copy-start(bf16[2,4,128,1024]{3,2,1,0:T(8,128)(2,1)} %param.7) | copy-start | bytes 6291460
  179.3 17.6 %copy-start.3 = (bf16[2,128,1024]{2,1,0:T(8,128)(2,1)S(1)}, bf16[2,128,1024]{2,1,0:T(8,128)(2,1)}, u32[]{:S(2)}) copy-start(bf16[2,128,1024]{2,1,0:T(8,128)(2,1)} %param.6) | copy-start | bytes 1572868
  182.2 90.0 %copy-start.2 = (bf16[2,4,128,1024]{3,2,1,0:T(8,128)(2,1)S(1)}, bf16[2,4,128,1024]{3,2,1,0:T(8,128)(2,1)}, u32[]{:S(2)}) copy-start(bf16[2,4,128,1024]{3,2,1,0:T(8,128)(2,1)} %param.7) | copy-start | bytes 6291460
  238.2 37.0 %copy-start.4 = (f32[2,128,32]{1,2,0:T(8,128)}, f32[2,128,32]{1,2,0:T(8,128)S(1)}, u32[]{:S(2)}) copy-start(f32[2,128,32]{1,2,0:T(8,128)S(1)} %fusion.40) | copy-start | bytes 98308
  238.2 8.3 %collective-permute-start.3 = (f32[2,128,32]{1,2,0:T(8,128)S(1)}, f32[2,128,32]{1,2,0:T(8,128)S(1)}, u32[]{:S(2)}, u32[]{:S(2)}) collective-permute-start(f32[2,128,32]{1,2,0:T(8,128)S(1)} %fusion.40), channel_id=1, source_target_pairs={{8,0},{16,8},{24,16},{32,24},{40,32},{48,40},{56,48},{64,56},{72,6... | collective-permute-start | bytes 98312 | tf_op jit(solution)/shard_map/ppermute | solution.py:18
  243.7 12.7 %collective-permute-start.2 = (f32[2,128,32]{1,2,0:T(8,128)S(1)}, f32[2,128,32]{1,2,0:T(8,128)S(1)}, u32[]{:S(2)}, u32[]{:S(2)}) collective-permute-start(f32[2,128,32]{1,2,0:T(8,128)S(1)} %fusion.40), channel_id=1, source_target_pairs={{0,8},{8,16},{16,24},{24,32},{32,40},{40,48},{48,56},{56,64},{64,7... | collective-permute-start | bytes 98312 | tf_op jit(solution)/shard_map/ppermute | solution.py:17
Sparse Core Ops, SparseCore 0:
  246.6 75.7 all-reduce.1
